TPU v7x, 256 devices: a whole 4x4x8 slice. The times are simulated.
256 devices in a mesh: tile: 64 (over z, x, core), mp: 4 (over y).
Axes of the slice: x: 4, y: 4, z: 8, core: 2. Of those that a mesh axis runs over, the one named last changes fastest.
Arguments:
- latent: bfloat16 [768, 384], P('tile'), may hold values from -19 to 19, as said below
- reward_grad: float32 [768, 384], P('tile'), may hold values from -6 to 6
- curvature: float32 [768, 384], P('tile'), may hold values from 0.3 to 3
- offsets: int32 [128, 2], P('tile'), may hold values from 0 to 736, as said below
- counts: int32 [768, 96], P('tile'), may hold values from 1 to 4, as said below
- w_in: bfloat16 [16, 640], replicated, may hold values from -3.2 to 3.2, as said below
- w_value: bfloat16 [640, 2560], P(None, 'mp'), may hold values from -0.25 to 0.25
- w_gate: bfloat16 [640, 2560], P(None, 'mp'), may hold values from -0.25 to 0.25
- w_down: bfloat16 [2560, 640], P('mp'), may hold values from -0.125 to 0.125
- w_out: bfloat16 [640, 16], replicated, may hold values from -0.25 to 0.25
Outputs:
- blended: float32 [768, 384], P('tile')
- grad_in: float32 [16, 640], replicated
- grad_value: float32 [640, 2560], P(None, 'mp')
- grad_gate: float32 [640, 2560], P(None, 'mp')
- grad_down: float32 [2560, 640], P('mp')
- grad_out: float32 [640, 16], replicated
Inputs may be any that keep to these rules, and one draw needn't show every extreme that they name: `offsets`: the corners are the points of a grid of 32 by 4 points spaced 24, each point taken by exactly one tile in a random order, each moved by at most 4 along each direction; the grid's first row and column stay at 0 and its last row and column are clamped to 736 and 64. The tiles cover every cell of the canvas. `counts`: the number of tiles whose 32 x 32 square holds the cell. `latent`: Real-valued. `w_in`: Real-valued.
All inputs are finite; a program needn't handle non-finite values.
Results may differ from a plain program's by a relative error of at most 0.003.
The roundings to bfloat16 on the way count: a program that leaves them out, or rounds other values in their place, can miss the bound.
Values may be sent and summed in bfloat16 or wider, within the bound.
A program may use at most 64 MiB of HBM per device.

v0:
```python
import math
import jax
import jax.numpy as jnp
from jax import lax
from jax.sharding import PartitionSpec as P

S = 32
layer_eps = 1e-05
root_half = 0.7071067811865476
inv_root_two_pi = 0.3989422804014327
highest = lax.Precision.HIGHEST


def gelu_value(inputs):
    return 0.5 * inputs * (1.0 + lax.erf(inputs * root_half))


def gelu_slope(inputs):
    return (
        0.5 * (1.0 + lax.erf(inputs * root_half))
        + inputs * jnp.exp(-0.5 * inputs * inputs) * inv_root_two_pi
    )


def patchify(cropped, channels):
    half_side = cropped.shape[0] // 2
    return (
        cropped.reshape(half_side, 2, half_side, 2 * channels)
        .transpose(0, 2, 1, 3)
        .reshape(half_side * half_side, 4 * channels)
    )


def unpatch(tokens, tile_side, channels):
    half_side = tile_side // 2
    token_rows = tokens.shape[0] // half_side
    return (
        tokens.reshape(token_rows, half_side, 2, 2 * channels)
        .transpose(0, 2, 1, 3)
        .reshape(2 * token_rows, tile_side * channels)
    )


def layer_norm(hidden):
    values = hidden.astype(jnp.float32)
    center = values - jnp.mean(values, axis=-1, keepdims=True)
    variance = jnp.mean(center * center, axis=-1, keepdims=True)
    inv_scale = lax.rsqrt(variance + layer_eps)
    return (center * inv_scale, inv_scale)


def norm_backward(normed, inv_scale, d_unit):
    centered = d_unit - jnp.mean(d_unit, axis=-1, keepdims=True)
    return inv_scale * (centered - normed * jnp.mean(d_unit * normed, axis=-1, keepdims=True))


def contract_rows(left, right):
    return lax.dot_general(
        left, right, (((0,), (0,)), ((), ())), preferred_element_type=jnp.float32
    )


def contract_rows_exact(left, right):
    return lax.dot_general(
        left, right, (((0,), (0,)), ((), ())), precision=highest, preferred_element_type=jnp.float32
    )


def contract_cols(left, right):
    return lax.dot_general(
        left, right, (((1,), (1,)), ((), ())), preferred_element_type=jnp.float32
    )


def crop_tiles(source, corners, tile_side, channels):

    def crop_one(corner):
        cropped = lax.dynamic_slice(
            source, (corner[0], corner[1] * channels), (tile_side, tile_side * channels)
        )
        return patchify(cropped, channels)

    return jax.vmap(crop_one)(corners)


def place_tiles(canvas, pieces, corners, row_shift, channels):
    piece_rows = pieces.shape[1]
    piece_cols = pieces.shape[2]

    def add_tile(tile_index, current):
        corner = corners[tile_index]
        start_row = corner[0] + row_shift
        start_col = corner[1] * channels
        existing = lax.dynamic_slice(current, (start_row, start_col), (piece_rows, piece_cols))
        return lax.dynamic_update_slice(
            current, existing + pieces[tile_index], (start_row, start_col)
        )

    return lax.fori_loop(0, pieces.shape[0], add_tile, canvas)


def per_device(
    latent, reward_grad, curvature, offsets, counts, w_in, w_value, w_gate, w_down, w_out
):
    channels = w_in.shape[0] // 4
    model_width = w_in.shape[1]
    tile_side = S
    half_side = tile_side // 2
    token_count = half_side * half_side
    tiles_here = offsets.shape[0]
    slab_rows = latent.shape[0]
    canvas_cols = latent.shape[1]
    tile_devices = lax.axis_size("tile")
    model_devices = lax.axis_size("mp")
    model_pos = lax.axis_index("mp")
    share_tokens = token_count // model_devices
    share_pixels = tile_side // model_devices
    scale_factor = 16.0 / math.sqrt(tiles_here * tile_devices * token_count)
    w_out_wide = w_out.astype(jnp.float32)
    cover_count = jnp.repeat(counts, channels, axis=1).astype(jnp.float32)
    placed_row = model_pos * share_pixels
    latent_source = lax.all_gather(latent, "tile", axis=0, tiled=True)
    patches = crop_tiles(latent_source, offsets, tile_side, channels)
    flat_patches = jnp.transpose(patches, (1, 0, 2)).reshape(token_count * tiles_here, 4 * channels)
    hidden = jnp.dot(flat_patches, w_in, preferred_element_type=jnp.float32).astype(jnp.bfloat16)
    normed, inv_scale = layer_norm(hidden)
    unit_in = normed.astype(jnp.bfloat16)
    value_proj = jnp.dot(unit_in, w_value, preferred_element_type=jnp.float32)
    gate_proj = jnp.dot(unit_in, w_gate, preferred_element_type=jnp.float32)
    active = (value_proj * gelu_value(gate_proj)).astype(jnp.bfloat16)
    active_grid = active.reshape(token_count, tiles_here, active.shape[1])

    def take_share(values):
        grid = values.reshape(token_count, tiles_here, values.shape[-1])
        picked = lax.dynamic_slice_in_dim(grid, model_pos * share_tokens, share_tokens, 0)
        return picked.reshape(share_tokens * tiles_here, values.shape[-1])

    hidden_share = take_share(hidden)
    row_block = active_grid.reshape(
        lax.axis_size("mp") * share_tokens * tiles_here, active_grid.shape[2]
    )
    ff_share = lax.psum_scatter(
        jnp.dot(row_block, w_down, preferred_element_type=jnp.float32).reshape(
            lax.axis_size("mp") * share_tokens, tiles_here, model_width
        ),
        "mp",
        scatter_dimension=0,
        tiled=True,
    ).reshape(share_tokens * tiles_here, model_width)
    noise_share = jnp.dot(hidden_share, w_out, preferred_element_type=jnp.float32) + jnp.dot(
        ff_share, w_out_wide, precision=highest, preferred_element_type=jnp.float32
    )
    noise_tiles = jnp.transpose(
        noise_share.reshape(share_tokens, tiles_here, w_out.shape[1]), (1, 0, 2)
    )

    def unpatch_share(tokens):
        return unpatch(tokens, tile_side, channels)

    noise_pieces = jax.vmap(unpatch_share)(noise_tiles)
    canvas_term = place_tiles(
        jnp.zeros((slab_rows * tile_devices, canvas_cols), jnp.float32),
        noise_pieces,
        offsets,
        placed_row,
        channels,
    )
    share_total = lax.psum_scatter(canvas_term, ("tile", "mp"), scatter_dimension=0, tiled=True)
    rows_each = slab_rows // model_devices
    first_share = model_pos * rows_each
    share_cover = lax.dynamic_slice_in_dim(cover_count, first_share, rows_each, 0)
    share_reward = lax.dynamic_slice_in_dim(reward_grad, first_share, rows_each, 0)
    share_curve = lax.dynamic_slice_in_dim(curvature, first_share, rows_each, 0)
    share_blend = share_total / share_cover
    share_cot = ((share_reward - share_curve * share_blend) / share_cover * scale_factor).astype(
        jnp.bfloat16
    )
    blended = lax.all_gather(share_blend, "mp", axis=0, tiled=True)
    cot_source = lax.all_gather(share_cot, ("tile", "mp"), axis=0, tiled=True)
    cot_patches = crop_tiles(cot_source, offsets, tile_side, channels)
    cot_flat = jnp.transpose(cot_patches, (1, 0, 2)).reshape(token_count * tiles_here, 4 * channels)
    cot_share = take_share(cot_flat)
    d_feat = contract_cols(cot_flat, w_out)
    d_feat_b = d_feat.astype(jnp.bfloat16)
    d_active = contract_cols(d_feat_b, w_down)
    down_term = contract_rows(active, d_feat_b)
    d_value = (d_active * gelu_value(gate_proj)).astype(jnp.bfloat16)
    d_gate = (d_active * value_proj * gelu_slope(gate_proj)).astype(jnp.bfloat16)
    value_term = contract_rows(unit_in, d_value)
    gate_term = contract_rows(unit_in, d_gate)
    d_value_grid = d_value.reshape(token_count, tiles_here, d_value.shape[1])
    d_gate_grid = d_gate.reshape(token_count, tiles_here, d_gate.shape[1])
    value_block = d_value_grid.reshape(
        share_tokens * lax.axis_size("mp") * tiles_here, d_value.shape[1]
    )
    gate_block = d_gate_grid.reshape(
        share_tokens * lax.axis_size("mp") * tiles_here, d_gate.shape[1]
    )
    summed = contract_cols(value_block, w_value) + contract_cols(gate_block, w_gate)
    d_unit_share = (
        lax.psum_scatter(
            summed.reshape(share_tokens * lax.axis_size("mp"), tiles_here, model_width).astype(
                jnp.bfloat16
            ),
            "mp",
            scatter_dimension=0,
            tiled=True,
        )
        .astype(jnp.float32)
        .reshape(share_tokens * tiles_here, model_width)
    )
    d_hidden = (
        take_share(d_feat) + norm_backward(take_share(normed), take_share(inv_scale), d_unit_share)
    ).astype(jnp.bfloat16)
    in_term = contract_rows(take_share(flat_patches), d_hidden)
    out_term = contract_rows(hidden_share, cot_share) + contract_rows_exact(
        ff_share, cot_share.astype(jnp.float32)
    )
    grad_in, grad_out = lax.psum((in_term, out_term), ("tile", "mp"))
    grad_value, grad_gate, grad_down = lax.psum((value_term, gate_term, down_term), "tile")
    return (blended, grad_in, grad_value, grad_gate, grad_down, grad_out)


def solution(mesh):
    return jax.shard_map(
        per_device,
        mesh=mesh,
        in_specs=(
            P("tile", None),
            P("tile", None),
            P("tile", None),
            P("tile", None),
            P("tile", None),
            P(),
            P(None, "mp"),
            P(None, "mp"),
            P("mp", None),
            P(),
        ),
        out_specs=(P("tile", None), P(), P(None, "mp"), P(None, "mp"), P("mp", None), P()),
        check_vma=False,
    )
```

profile of v0, /device:TPU:97, one launch (start us, length us, event | category | flops | bytes accessed | tf_op | source)
XLA Modules:
  0.0 971.2 jit_solution(10086862064302789510)
XLA Ops:
  8.1 51.5 %all-gather = bf16[64,12,384]{2,1,0:T(8,128)(2,1)S(1)} all-gather(bf16[1,12,384]{2,1,0:T(8,128)(2,1)} %bitcast.107), channel_id=1, replica_groups=mesh['tile'=64,'mp'=4] {'tile'}, dimensions={0}, use_global_device_ids=true | all-gather | bytes 599040 | tf_op jit(solution)/shard_map/all_gather | solution.py:122
  59.8 4.0 while.16
  66.5 1.9 multiply_convert_fusion.1
  69.2 1.8 reshape.143
  73.2 48.7 %all-reduce.9.cloned.1.call-done = f32[256,2,640]{2,1,0:T(2,128)} async-done(((f32[256,2,640]{2,1,0:T(2,128)}), f32[256,2,640]{2,1,0:T(2,128)}) %all-reduce.9.cloned.1.call-update) | async-done | bytes 1310736
  124.1 5.1 while.15
  133.9 259.7 %all-reduce.11.cloned.1.call-done = f32[768,384]{0,1:T(8,128)} async-done(((f32[768,384]{0,1:T(8,128)}), f32[768,384]{0,1:T(8,128)}) %all-reduce.11.cloned.1.call-update) | async-done | bytes 1179664
  393.6 1.9 fusion.23
  395.6 70.2 %all-gather.2 = bf16[256,3,384]{2,1,0:T(4,128)(2,1)S(1)} all-gather(bf16[1,3,384]{2,1,0:T(4,128)(2,1)S(1)} %copy.75), channel_id=1, replica_groups=mesh['tile'=64,'mp'=4] {'tile','mp'}, dimensions={0}, use_global_device_ids=true | all-gather | bytes 592128 | tf_op jit(solution)/shard_map/all_gather | solution.py:179
  466.3 4.0 while.17
  473.0 2.9 fusion.9
  479.1 2.6 convert_element_type.57
  481.7 2.0 copy.80
  484.7 2.9 reshape.152
  489.4 1.8 reshape.151
  496.0 3.1 fusion.35
  499.2 1.9 fusion.17
  501.0 4.6 reduce-scatter.3.cloned.1.call-done
  506.8 2.1 convolution_bitcast_fusion.2
  509.0 2.0 fusion.37
  512.0 9.1 all-gather.1
  521.7 235.5 %all-reduce.13.cloned.1.call-done = (f32[16,640]{1,0:T(8,128)}, f32[640,16]{0,1:T(8,128)}) async-done(((f32[16,640]{1,0:T(8,128)}, f32[640,16]{0,1:T(8,128)}), (f32[16,640]{1,0:T(8,128)}, f32[640,16]{0,1:T(8,128)})) %all-reduce.13.cloned.1.call-update) | async-done | bytes 81936 | tf_op jit(solution)/shard_map/psum | solution.py:219
  757.3 199.4 %all-reduce.15.cloned.1.call-done = (f32[640,640]{1,0:T(8,128)}, f32[640,640]{1,0:T(8,128)}, f32[640,640]{1,0:T(8,128)}) async-done(((f32[640,640]{1,0:T(8,128)}, f32[640,640]{1,0:T(8,128)}, f32[640,640]{1,0:T(8,128)}), (f32[640,640]{1,0:T(8,128)}, f32[640,640]{1,0:T(8,128)}, f32[640,640]{1,0:T(8,128)})) %all-reduce.15.cloned.1.call-update) | async-done | bytes 4915216 | tf_op jit(solution)/shard_map/psum | solution.py:220
  958.0 2.8 copy.130
  (132 shorter events, 45.1 us)
Async XLA Ops:
  7.2 61.2 %copy-start = (bf16[640,640]{1,0:T(8,128)(2,1)S(1)}, bf16[640,640]{1,0:T(8,128)(2,1)}, u32[]{:S(2)}) copy-start(bf16[640,640]{1,0:T(8,128)(2,1)} %param.20) | copy-start | bytes 2457604
  7.2 114.7 %all-reduce.9.cloned.1.call-start = ((), (), s32[]{:S(2)}) async-start(), calls=%async_computation.2 | async-start | bytes 2621440
  59.6 5.0 copy-start.16
  59.8 5.6 copy-start.11
  65.4 1.1 copy-start.1
  66.5 1.9 copy-start.10
  71.0 2.0 copy-start.14
  71.0 322.6 %all-reduce.11.cloned.1.call-start = ((), (), s32[]{:S(2)}) async-start(), calls=%async_computation.3 | async-start | bytes 2359296
  71.5 1.7 copy-start.9
  122.9 1.0 copy-start.3
  122.9 1.1 copy-start.18
  129.2 2.3 copy-start.17
  130.6 375.0 %reduce-scatter.3.cloned.1.call-start = ((), (), s32[]{:S(2)}) async-start(), calls=%async_computation.1 | async-start | bytes 819200 | tf_op jit(solution)/shard_map/reduce_scatter | solution.py:201
  473.0 2.9 copy-start.2
  475.8 0.9 copy-start.4
  475.9 1.1 copy-start.6
  475.9 1.6 copy-start.12
  483.8 273.5 %all-reduce.13.cloned.1.call-start = ((), (), s32[]{:S(2)}) async-start(), calls=%async_computation.4 | async-start | bytes 163840 | tf_op jit(solution)/shard_map/psum | solution.py:219
  501.0 7.9 copy-start.5
  508.9 447.7 %all-reduce.15.cloned.1.call-start = ((), (), s32[]{:S(2)}) async-start(), calls=%async_computation.5 | async-start | bytes 9830400 | tf_op jit(solution)/shard_map/psum | solution.py:220
  511.0 0.9 copy-start.13
  958.0 2.8 copy-start.8
  960.9 2.0 copy-start.7
  962.9 1.2 copy-start.15
  (1 other events, 0.7 us)
Sparse Core Ops, SparseCore 0:
  71.1 50.6 all-reduce.8
  130.7 262.8 all-reduce.10
  483.9 21.6 reduce-scatter.2
  511.7 245.4 all-reduce.12
  761.6 195.0 all-reduce.14
where the time goes:
time: 972 us; the launch traced here: 971 us
  waiting for transfers between devices  748 us (77%)
  blocking collectives  131 us (13%)
  local copies, waits for them, and re-layouts  45.9 us (5%)
  matrix products  22.9 us (2%)
  between operations  14.9 us (2%)
    unnamed x7, waiting for transfers between devices  309 us
    psum x1, waiting for transfers between devices, per_device(): grad_in, grad_out = lax.psum((in_term, out_term), ('tile', 'mp'))  236 us
    psum x1, waiting for transfers between devices, per_device(): lax.psum((value_term, gate_term, down_term), 'tile')  199 us
    all_gather x1, blocking collectives, per_device(): cot_source = lax.all_gather(share_cot, ('tile', 'mp'), axis=0, tiled=True)  70.2 us
    all_gather x1, blocking collectives, per_device(): latent_source = lax.all_gather(latent, 'tile', axis=0, tiled=True)  51.5 us
  transfers between devices with their start and end apart: 5, of which 5 were waited for; matrix products, arithmetic and copies ran while one was open for 3% of the time, Pallas kernels for 0%

commit v1 on v0

--- a/solution.py
+++ b/solution.py
@@ -176,7 +176,12 @@
         jnp.bfloat16
     )
     blended = lax.all_gather(share_blend, "mp", axis=0, tiled=True)
-    cot_source = lax.all_gather(share_cot, ("tile", "mp"), axis=0, tiled=True)
+    cot_source = jnp.concatenate(
+        lax.all_to_all(
+            jnp.stack([share_cot] * lax.axis_size(("tile", "mp"))), ("tile", "mp"), 0, 0
+        ),
+        axis=0,
+    )
     cot_patches = crop_tiles(cot_source, offsets, tile_side, channels)
     cot_flat = jnp.transpose(cot_patches, (1, 0, 2)).reshape(token_count * tiles_here, 4 * channels)
     cot_share = take_share(cot_flat)

time: 972 us -> 934 us (0.961)
  blocking collectives: 131 us -> 60.6 us
  waiting for transfers between devices: 748 us -> 770 us
    all_gather x1 -> x0, blocking collectives: 70.2 us -> none  [per_device(): cot_source = lax.all_gather(share_cot, ('tile', 'mp'), axis=0, tiled=True)]
    all_to_all x0 -> x1, waiting for transfers between devices: none -> 20.8 us  [per_device(): lax.all_to_all(jnp.stack([share_cot] * lax.axis_size(('tile', 'mp'))), ('...]
  transfers between devices with their start and end apart: 5 -> 6, of which waited for: 5 -> 6; matrix products, arithmetic and copies ran while one was open for 3% -> 3% of each run, Pallas kernels for 0% -> 0%
where the time goes in v1:
time: 934 us; the launch traced here: 933 us
  waiting for transfers between devices  770 us (82%)
  blocking collectives  60.6 us (6%)
  local copies, waits for them, and re-layouts  47 us (5%)
  matrix products  22.9 us (2%)
  between operations  14.8 us (2%)
  starting transfers between devices  9.73 us (1%)
    unnamed x7, waiting for transfers between devices  312 us
    psum x1, waiting for transfers between devices, per_device(): grad_in, grad_out = lax.psum((in_term, out_term), ('tile', 'mp'))  236 us
    psum x1, waiting for transfers between devices, per_device(): lax.psum((value_term, gate_term, down_term), 'tile')  199 us
    all_gather x1, blocking collectives, per_device(): latent_source = lax.all_gather(latent, 'tile', axis=0, tiled=True)  51.5 us
    all_to_all x1, waiting for transfers between devices, per_device(): lax.all_to_all(jnp.stack([share_cot] * lax.axis_size(('tile', 'mp'))), ('...  20.8 us
  transfers between devices with their start and end apart: 6, of which 6 were waited for; matrix products, arithmetic and copies ran while one was open for 3% of the time, Pallas kernels for 0%

profile of v1, /device:TPU:97, one launch (start us, length us, event | category | flops | bytes accessed | tf_op | source)
XLA Modules:
  0.0 932.6 jit_solution(6358419212517309448)
XLA Ops:
  8.1 51.5 %all-gather = bf16[64,12,384]{2,1,0:T(8,128)(2,1)S(1)} all-gather(bf16[1,12,384]{2,1,0:T(8,128)(2,1)} %bitcast.105), channel_id=1, replica_groups=mesh['tile'=64,'mp'=4] {'tile'}, dimensions={0}, use_global_device_ids=true | all-gather | bytes 599040 | tf_op jit(solution)/shard_map/all_gather | solution.py:122
  59.8 4.0 while.16
  66.5 1.9 multiply_convert_fusion.1
  69.2 1.8 reshape.148
  73.1 48.8 %all-reduce.9.cloned.1.call-done = f32[256,2,640]{2,1,0:T(2,128)} async-done(((f32[256,2,640]{2,1,0:T(2,128)}), f32[256,2,640]{2,1,0:T(2,128)}) %all-reduce.9.cloned.1.call-update) | async-done | bytes 1310736
  124.1 5.1 while.15
  130.9 262.6 %all-reduce.11.cloned.1.call-done = f32[768,384]{0,1:T(8,128)} async-done(((f32[768,384]{0,1:T(8,128)}), f32[768,384]{0,1:T(8,128)}) %all-reduce.11.cloned.1.call-update) | async-done | bytes 1179664
  397.3 9.3 %all-to-all-start = ((bf16[256,3,384]{2,1,0:T(4,128)(2,1)}), bf16[256,3,384]{2,1,0:T(4,128)(2,1)S(1)}, u32[]{:S(2)}, u32[]{:S(2)}) async-start(bf16[256,3,384]{2,1,0:T(4,128)(2,1)} %stack.2), calls=%async_computation | async-start | bytes 1572864 | tf_op jit(solution)/shard_map/all_to_all | solution.py:180
  408.9 20.8 %all-to-all-done = bf16[256,3,384]{2,1,0:T(4,128)(2,1)S(1)} async-done(((bf16[256,3,384]{2,1,0:T(4,128)(2,1)}), bf16[256,3,384]{2,1,0:T(4,128)(2,1)S(1)}, u32[]{:S(2)}, u32[]{:S(2)}) %all-to-all-start) | async-done | bytes 589856 | tf_op jit(solution)/shard_map/all_to_all | solution.py:180
  430.3 4.0 while.17
  437.0 2.9 fusion.9
  443.1 2.6 convert_element_type.57
  445.7 2.0 copy.98
  448.7 2.9 reshape.158
  453.4 1.8 reshape.157
  460.1 3.1 fusion.33
  463.2 1.9 fusion.17
  465.1 2.1 reduce-scatter.3.cloned.1.call-done
  468.4 2.1 convolution_bitcast_fusion.2
  470.5 2.0 fusion.35
  473.3 9.1 all-gather.1
  483.0 235.7 %all-reduce.13.cloned.1.call-done = (f32[16,640]{1,0:T(8,128)}, f32[640,16]{0,1:T(8,128)}) async-done(((f32[16,640]{1,0:T(8,128)}, f32[640,16]{0,1:T(8,128)}), (f32[16,640]{1,0:T(8,128)}, f32[640,16]{0,1:T(8,128)})) %all-reduce.13.cloned.1.call-update) | async-done | bytes 81936 | tf_op jit(solution)/shard_map/psum | solution.py:224
  718.7 199.4 %all-reduce.15.cloned.1.call-done = (f32[640,640]{1,0:T(8,128)}, f32[640,640]{1,0:T(8,128)}, f32[640,640]{1,0:T(8,128)}) async-done(((f32[640,640]{1,0:T(8,128)}, f32[640,640]{1,0:T(8,128)}, f32[640,640]{1,0:T(8,128)}), (f32[640,640]{1,0:T(8,128)}, f32[640,640]{1,0:T(8,128)}, f32[640,640]{1,0:T(8,128)})) %all-reduce.15.cloned.1.call-update) | async-done | bytes 4915216 | tf_op jit(solution)/shard_map/psum | solution.py:225
  919.4 2.8 copy.147
  (132 shorter events, 47.7 us)
Async XLA Ops:
  7.2 61.2 %copy-start = (bf16[640,640]{1,0:T(8,128)(2,1)S(1)}, bf16[640,640]{1,0:T(8,128)(2,1)}, u32[]{:S(2)}) copy-start(bf16[640,640]{1,0:T(8,128)(2,1)} %param.20) | copy-start | bytes 2457604
  7.2 114.7 %all-reduce.9.cloned.1.call-start = ((), (), s32[]{:S(2)}) async-start(), calls=%async_computation.3 | async-start | bytes 2621440
  59.6 5.0 copy-start.16
  59.8 5.6 copy-start.11
  65.4 1.1 copy-start.1
  66.5 1.9 copy-start.10
  71.0 1.9 copy-start.13
  71.0 322.5 %all-reduce.11.cloned.1.call-start = ((), (), s32[]{:S(2)}) async-start(), calls=%async_computation.4 | async-start | bytes 2359296
  71.5 1.6 copy-start.9
  122.9 1.0 copy-start.3
  122.9 1.1 copy-start.18
  129.1 1.4 copy-start.17
  397.3 32.5 %all-to-all-start = ((bf16[256,3,384]{2,1,0:T(4,128)(2,1)}), bf16[256,3,384]{2,1,0:T(4,128)(2,1)S(1)}, u32[]{:S(2)}, u32[]{:S(2)}) async-start(bf16[256,3,384]{2,1,0:T(4,128)(2,1)} %stack.2), calls=%async_computation | async-start | bytes 1572864 | tf_op jit(solution)/shard_map/all_to_all | solution.py:180
  406.6 60.6 %reduce-scatter.3.cloned.1.call-start = ((), (), s32[]{:S(2)}) async-start(), calls=%async_computation.2 | async-start | bytes 819200 | tf_op jit(solution)/shard_map/reduce_scatter | solution.py:206
  437.0 2.9 copy-start.2
  439.8 0.8 copy-start.4
  439.8 1.1 copy-start.6
  439.9 1.6 copy-start.12
  447.8 270.9 %all-reduce.13.cloned.1.call-start = ((), (), s32[]{:S(2)}) async-start(), calls=%async_computation.5 | async-start | bytes 163840 | tf_op jit(solution)/shard_map/psum | solution.py:224
  465.1 5.4 copy-start.5
  470.5 447.6 %all-reduce.15.cloned.1.call-start = ((), (), s32[]{:S(2)}) async-start(), calls=%async_computation.6 | async-start | bytes 9830400 | tf_op jit(solution)/shard_map/psum | solution.py:225
  919.4 2.8 copy-start.8
  922.3 2.0 copy-start.7
  924.3 1.2 copy-start.14
  (2 other events, 1.4 us)
Sparse Core Ops, SparseCore 0:
  71.1 50.6 all-reduce.8
  130.7 262.8 all-reduce.10
  447.9 19.2 reduce-scatter.2
  473.3 245.3 all-reduce.12
  723.0 195.0 all-reduce.14
